TPU v7x, 256 devices: a whole 4x4x8 slice. The times are simulated.
256 devices in a mesh: grp: 8 (over z_lo, x), dev: 32 (over z_hi, y, core).
Axes of the slice: x: 4, y: 4, z: 8 (z_hi: 4, z_lo: 2; z = z_hi * 2 + z_lo), core: 2. Of those that a mesh axis runs over, the one named last changes fastest.
Arguments:
- pair_ft: bfloat16 [8192, 2, 4096], P('dev', None, 'grp'), may hold values from -6 to 6
- aux_ft: bfloat16 [4096, 2, 4096], P('dev', None, 'grp'), may hold values from -0.0625 to 0.0625
- coul_weight: float32 [4096], P('grp'), may hold values from 0.2 to 5
- aux_basis: bfloat16 [128, 4096], replicated, may hold values from -0.5 to 0.5
- aux_decay: float32 [4096], replicated, may hold values from 0.05 to 1
- image_dist: float32 [125], replicated, may hold values from 0 to 3
- image_phase: float32 [125], replicated, may hold values from -3.140625 to 3.140625
- item_pair: bfloat16 [4096, 128, 128], P(('grp', 'dev')), may hold values from -4 to 4
- item_image: int32 [4096], P(('grp', 'dev')), may hold values from 0 to 124
- item_sub: int32 [4096], P(('grp', 'dev')), may hold values from 0 to 1
- item_count: int32 [256], P(('grp', 'dev')), may hold values from 0 to 16, as said below
Outputs:
- j3c: bfloat16 [4096, 2, 8192], P('grp', None, 'dev')
Inputs may be any that keep to these rules, and one draw needn't show every extreme that they name: `item_count`: in every index of dev one of the 8 devices holds exactly 16 live slots. The counts of the 8 devices that share an index of dev sum to at most 72, and in every draw some index of dev reaches 72.
All inputs are finite; a program needn't handle non-finite values.
Results may differ from a plain program's by a relative error of at most 0.0047.
Values may be sent and summed in bfloat16 or wider, within the bound.
A program may use at most 64 MiB of HBM per device.

v0:
```python
import math
import jax
import jax.numpy as jnp
from jax import lax
from jax.sharding import PartitionSpec as P


def stacked_pairs(weighted):
    real_part = weighted[:, 0, :].T
    imag_part = weighted[:, 1, :].T
    real_cols = jnp.concatenate([real_part, imag_part], axis=0)
    imag_cols = jnp.concatenate([imag_part, -real_part], axis=0)
    return jnp.concatenate([real_cols, imag_cols], axis=1)


def short_range(
    aux_basis,
    aux_decay,
    image_dist,
    image_phase,
    first_row,
    row_count,
    blocks,
    images,
    sub_ids,
    usable,
    sub_count,
):
    basis_cols = lax.dynamic_slice_in_dim(aux_basis, first_row, row_count, 1)
    decay_rows = lax.dynamic_slice_in_dim(aux_decay, first_row, row_count, 0)
    products = jnp.einsum("kp,ikr->pir", basis_cols, blocks, preferred_element_type=jnp.float32)
    lookup = (images[:, None] == jnp.arange(image_dist.shape[0], dtype=jnp.int32)[None, :]).astype(
        jnp.float32
    )
    distance = jnp.dot(lookup, image_dist, precision=lax.Precision.HIGHEST)
    phase_value = jnp.dot(lookup, image_phase, precision=lax.Precision.HIGHEST)
    damping = jnp.exp(-decay_rows[:, None] * distance[None, :])
    factors = jnp.stack([jnp.cos(phase_value) * usable, jnp.sin(phase_value) * usable], axis=0)
    weights = damping[:, None, :] * factors[None, :, :]
    placing = (sub_ids[:, None] == jnp.arange(sub_count, dtype=jnp.int32)[None, :]).astype(
        jnp.float32
    )
    placed = jnp.einsum(
        "pir,pci,is->pcsr", products, weights, placing, precision=lax.Precision.HIGHEST
    )
    return placed.reshape(row_count, 2, sub_count * products.shape[2])


def body(
    pair_ft,
    aux_ft,
    coul_weight,
    aux_basis,
    aux_decay,
    image_dist,
    image_phase,
    item_pair,
    item_image,
    item_sub,
    item_count,
):
    group_count = lax.axis_size("grp")
    member_count = lax.axis_size("dev")
    capacity = item_image.shape[0]
    local_rows = pair_ft.shape[0]
    sub_rows = item_pair.shape[2]
    sub_count = local_rows // sub_rows
    aux_share = aux_ft.shape[0] * member_count // group_count
    weighted = (pair_ft.astype(jnp.float32) * coul_weight[None, None, :]).astype(jnp.bfloat16)

    def make_term(factors, factor_offset, pair_matrix, blocks, images, sub_ids, usable):

        def term_rows(first_row, row_count):
            block_rows = math.gcd(row_count, 512)

            def one_block(block_index):
                block_start = block_index * block_rows
                local_factors = lax.dynamic_slice_in_dim(
                    factors, block_start - factor_offset, block_rows, 0
                )
                factor_rows = local_factors.reshape(block_rows, -1)
                long_part = jnp.dot(factor_rows, pair_matrix, preferred_element_type=jnp.float32)
                long_part = long_part.reshape(block_rows, 2, local_rows)
                return long_part + short_range(
                    aux_basis,
                    aux_decay,
                    image_dist,
                    image_phase,
                    block_start,
                    block_rows,
                    blocks,
                    images,
                    sub_ids,
                    usable,
                    sub_count,
                )

            pieces = lax.map(one_block, jnp.arange(row_count // block_rows, dtype=jnp.int32))
            return pieces.reshape(row_count, 2, local_rows)

        return term_rows

    gathered = lax.all_gather(aux_ft, "dev", axis=0, tiled=True)
    blocks = item_pair
    images = item_image
    sub_ids = item_sub
    usable = jnp.arange(capacity, dtype=jnp.int32) < item_count[0]
    term_rows = make_term(
        gathered, 0, stacked_pairs(weighted), blocks, images, sub_ids, usable.astype(jnp.float32)
    )
    summed = lax.psum_scatter(
        term_rows(jnp.int32(0), aux_share * lax.axis_size("grp")),
        "grp",
        scatter_dimension=0,
        tiled=True,
    )
    return summed.astype(jnp.bfloat16)


def solution(mesh):
    return jax.shard_map(
        body,
        mesh=mesh,
        in_specs=(
            P("dev", None, "grp"),
            P("dev", None, "grp"),
            P("grp"),
            P(),
            P(),
            P(),
            P(),
            P(("grp", "dev"), None, None),
            P(("grp", "dev")),
            P(("grp", "dev")),
            P(("grp", "dev")),
        ),
        out_specs=P("grp", None, "dev"),
        check_vma=False,
    )
```

profile of v0, /device:TPU:8, one launch (start us, length us, event | category | flops | bytes accessed | tf_op | source)
XLA Modules:
  0.0 434.1 jit_solution(11790446058027590612)
XLA Ops:
  7.9 1.3 dynamic-slice
  9.8 0.9 fusion.14
  10.7 0.9 convolution_bitcast_fusion.2
  11.5 1.1 multiply_convert_fusion
  12.8 1.1 maximum_maximum_fusion
  13.8 75.5 %all-gather.2.cloned.1.call-done = bf16[4096,2,512]{2,1,0:T(2,128)(2,1)} async-done(((bf16[128,2,512]{2,1,0:T(2,128)(2,1)}), bf16[4096,2,512]{2,1,0:T(2,128)(2,1)}) %all-gather.2.cloned.1.call-update) | async-done | bytes 8388624 | tf_op jit(solution)/shard_map/all_gather | solution.py:103
  89.3 161.8 %while.14 = (s32[]{:T(128)}, f32[8,512,2,256]{3,2,1,0:T(2,128)}, s32[8]{0:T(128)S(1)}, bf16[4096,2,512]{2,1,0:T(2,128)(2,1)}, bf16[1024,512]{0,1:T(8,128)(2,1)},...) while((s32[]{:T(128)}, f32[8,512,2,256]{3,2,1,0:T(2,128)}, ...), condition=%wide.region_1.2_spmd, body=%wide.region_0.1_spmd.sunk | while | flops 855958080 | bytes 25042132 | solution.py:98
  90.6 0.8 dynamic-slice_negate_fusion.2
  91.8 1.8 convolution_bitcast_fusion.4
  93.6 8.0 %fusion.38 = f32[512,2,2,128]{3,1,2,0:T(2,128)S(1)} fusion(f32[512,16,128,1]{2,0,1,3:T(8,128)S(1)} %convolution_bitcast_fusion.4, f32[16,512,2]{0,2,1:T(2,128)S(1)} %multiply_bitcast_fusion.2, f32[16,2]{0,1:T(2,128)S(1)} %compare_convert_fusion.2), kind=kOutput, calls=%fused_computation.3.clone.1 | convolution fusion | flops 50364416 | bytes 5308544 | tf_op jit(solution)/shard_map/while/body/eval_jaxpr/pir,pci,is->pcsr/dot_general | solution.py:43
  102.2 0.8 reshape.86
  103.0 2.0 constant_dynamic-slice_fusion.2
  105.8 2.0 fusion.39
  107.8 1.9 copy_dynamic-update-slice_fusion.2
  110.9 0.8 dynamic-slice_negate_fusion.2
  112.0 1.8 convolution_bitcast_fusion.4
  113.9 8.0 %fusion.38 = f32[512,2,2,128]{3,1,2,0:T(2,128)S(1)} fusion(f32[512,16,128,1]{2,0,1,3:T(8,128)S(1)} %convolution_bitcast_fusion.4, f32[16,512,2]{0,2,1:T(2,128)S(1)} %multiply_bitcast_fusion.2, f32[16,2]{0,1:T(2,128)S(1)} %compare_convert_fusion.2), kind=kOutput, calls=%fused_computation.3.clone.1 | convolution fusion | flops 50364416 | bytes 5308544 | tf_op jit(solution)/shard_map/while/body/eval_jaxpr/pir,pci,is->pcsr/dot_general | solution.py:43
  122.5 0.8 reshape.86
  123.3 2.0 constant_dynamic-slice_fusion.2
  126.0 2.0 fusion.39
  128.0 1.8 copy_dynamic-update-slice_fusion.2
  131.0 0.8 dynamic-slice_negate_fusion.2
  132.2 1.8 convolution_bitcast_fusion.4
  134.1 8.0 %fusion.38 = f32[512,2,2,128]{3,1,2,0:T(2,128)S(1)} fusion(f32[512,16,128,1]{2,0,1,3:T(8,128)S(1)} %convolution_bitcast_fusion.4, f32[16,512,2]{0,2,1:T(2,128)S(1)} %multiply_bitcast_fusion.2, f32[16,2]{0,1:T(2,128)S(1)} %compare_convert_fusion.2), kind=kOutput, calls=%fused_computation.3.clone.1 | convolution fusion | flops 50364416 | bytes 5308544 | tf_op jit(solution)/shard_map/while/body/eval_jaxpr/pir,pci,is->pcsr/dot_general | solution.py:43
  142.7 0.8 reshape.86
  143.5 2.0 constant_dynamic-slice_fusion.2
  146.2 2.0 fusion.39
  148.2 1.8 copy_dynamic-update-slice_fusion.2
  151.3 0.8 dynamic-slice_negate_fusion.2
  152.4 1.8 convolution_bitcast_fusion.4
  154.3 8.0 %fusion.38 = f32[512,2,2,128]{3,1,2,0:T(2,128)S(1)} fusion(f32[512,16,128,1]{2,0,1,3:T(8,128)S(1)} %convolution_bitcast_fusion.4, f32[16,512,2]{0,2,1:T(2,128)S(1)} %multiply_bitcast_fusion.2, f32[16,2]{0,1:T(2,128)S(1)} %compare_convert_fusion.2), kind=kOutput, calls=%fused_computation.3.clone.1 | convolution fusion | flops 50364416 | bytes 5308544 | tf_op jit(solution)/shard_map/while/body/eval_jaxpr/pir,pci,is->pcsr/dot_general | solution.py:43
  162.9 0.8 reshape.86
  163.7 2.0 constant_dynamic-slice_fusion.2
  166.4 2.0 fusion.39
  168.4 1.8 copy_dynamic-update-slice_fusion.2
  171.5 0.8 dynamic-slice_negate_fusion.2
  172.7 1.8 convolution_bitcast_fusion.4
  174.5 8.0 %fusion.38 = f32[512,2,2,128]{3,1,2,0:T(2,128)S(1)} fusion(f32[512,16,128,1]{2,0,1,3:T(8,128)S(1)} %convolution_bitcast_fusion.4, f32[16,512,2]{0,2,1:T(2,128)S(1)} %multiply_bitcast_fusion.2, f32[16,2]{0,1:T(2,128)S(1)} %compare_convert_fusion.2), kind=kOutput, calls=%fused_computation.3.clone.1 | convolution fusion | flops 50364416 | bytes 5308544 | tf_op jit(solution)/shard_map/while/body/eval_jaxpr/pir,pci,is->pcsr/dot_general | solution.py:43
  183.1 0.8 reshape.86
  183.9 2.0 constant_dynamic-slice_fusion.2
  186.7 2.0 fusion.39
  188.6 1.8 copy_dynamic-update-slice_fusion.2
  191.7 0.8 dynamic-slice_negate_fusion.2
  192.9 1.8 convolution_bitcast_fusion.4
  194.8 8.0 %fusion.38 = f32[512,2,2,128]{3,1,2,0:T(2,128)S(1)} fusion(f32[512,16,128,1]{2,0,1,3:T(8,128)S(1)} %convolution_bitcast_fusion.4, f32[16,512,2]{0,2,1:T(2,128)S(1)} %multiply_bitcast_fusion.2, f32[16,2]{0,1:T(2,128)S(1)} %compare_convert_fusion.2), kind=kOutput, calls=%fused_computation.3.clone.1 | convolution fusion | flops 50364416 | bytes 5308544 | tf_op jit(solution)/shard_map/while/body/eval_jaxpr/pir,pci,is->pcsr/dot_general | solution.py:43
  203.4 0.8 reshape.86
  204.2 2.0 constant_dynamic-slice_fusion.2
  206.9 2.0 fusion.39
  208.9 1.8 copy_dynamic-update-slice_fusion.2
  213.1 1.9 convolution_bitcast_fusion.4
  215.0 8.0 %fusion.38 = f32[512,2,2,128]{3,1,2,0:T(2,128)S(1)} fusion(f32[512,16,128,1]{2,0,1,3:T(8,128)S(1)} %convolution_bitcast_fusion.4, f32[16,512,2]{0,2,1:T(2,128)S(1)} %multiply_bitcast_fusion.2, f32[16,2]{0,1:T(2,128)S(1)} %compare_convert_fusion.2), kind=kOutput, calls=%fused_computation.3.clone.1 | convolution fusion | flops 50364416 | bytes 5308544 | tf_op jit(solution)/shard_map/while/body/eval_jaxpr/pir,pci,is->pcsr/dot_general | solution.py:43
  223.6 0.8 reshape.86
  224.4 2.0 constant_dynamic-slice_fusion.2
  227.1 2.0 fusion.39
  229.1 1.8 copy_dynamic-update-slice_fusion.2
  232.2 0.8 dynamic-slice_negate_fusion.2
  233.4 1.8 convolution_bitcast_fusion.4
  235.2 8.0 %fusion.38 = f32[512,2,2,128]{3,1,2,0:T(2,128)S(1)} fusion(f32[512,16,128,1]{2,0,1,3:T(8,128)S(1)} %convolution_bitcast_fusion.4, f32[16,512,2]{0,2,1:T(2,128)S(1)} %multiply_bitcast_fusion.2, f32[16,2]{0,1:T(2,128)S(1)} %compare_convert_fusion.2), kind=kOutput, calls=%fused_computation.3.clone.1 | convolution fusion | flops 50364416 | bytes 5308544 | tf_op jit(solution)/shard_map/while/body/eval_jaxpr/pir,pci,is->pcsr/dot_general | solution.py:43
  243.8 0.8 reshape.86
  244.7 2.0 constant_dynamic-slice_fusion.2
  247.4 2.0 fusion.39
  249.4 1.8 copy_dynamic-update-slice_fusion.2
  251.2 173.9 %all-reduce.2 = bf16[4096,2,256]{2,1,0:T(2,128)(2,1)} all-reduce(f32[4096,2,256]{2,1,0:T(2,128)} %bitcast.74), channel_id=2, replica_groups=mesh['grp'=8,'dev'=32] {'grp'}, use_global_device_ids=true, to_apply=%region_2.3.clone | all-reduce | flops 2097152 | bytes 12582912
  425.0 2.2 dynamic-slice_convert_fusion
  (68 shorter events, 19.9 us)
Async XLA Ops:
  6.5 3.2 copy-start
  6.5 82.8 %copy-start.1 = (s32[16]{0:T(128)S(1)}, s32[16]{0:T(128)}, u32[]{:S(2)}) copy-start(s32[16]{0:T(128)} %param.22) | copy-start | bytes 196
  6.5 82.8 %all-gather.2.cloned.1.call-start = ((), (), s32[]{:S(2)}) async-start(), calls=%async_computation | async-start | bytes 8650752 | tf_op jit(solution)/shard_map/all_gather | solution.py:103
Sparse Core Ops, SparseCore 0:
  9.9 79.3 all-gather.1
where the time goes:
time: 435 us; the launch traced here: 434 us
  blocking collectives  174 us (40%)
  matrix products  96.5 us (22%)
  waiting for transfers between devices  76.2 us (18%)
  local copies, waits for them, and re-layouts  56.5 us (13%)
  between operations  14.7 us (3%)
  other arithmetic  10.5 us (2%)
  loops' own time  5.75 us (1%)
    unnamed x1, blocking collectives  174 us
    all_gather x1, waiting for transfers between devices, body(): gathered = lax.all_gather(aux_ft, 'dev', axis=0, tiled=True)  75.5 us
    dot_general x8, matrix products, short_range(): jnp.einsum('pir,pci,is->pcsr', products, weights, placing, precision=lax....  64.2 us
    dot_general x8, matrix products, one_block(): jnp.dot(factor_rows, pair_matrix, preferred_element_type=jnp.float32)  15.8 us
    dynamic_slice x8, local copies, waits for them, and re-layouts, one_block(): lax.dynamic_slice_in_dim(factors, block_start - factor_offset, block_rows...  15.6 us
    dot_general x8, matrix products, short_range(): jnp.einsum('kp,ikr->pir', basis_cols, blocks, preferred_element_type=jnp....  14.8 us
    dynamic_update_slice x8, local copies, waits for them, and re-layouts, term_rows(): lax.map(one_block, jnp.arange(row_count // block_rows, dtype=jnp.int32))  14.5 us
  transfers between devices with their start and end apart: 1, of which 1 were waited for; matrix products, arithmetic and copies ran while one was open for 1% of the time, Pallas kernels for 0%

commit v1 on v0

--- a/solution.py
+++ b/solution.py
@@ -100,7 +100,8 @@
 
         return term_rows
 
-    gathered = lax.all_gather(aux_ft, "dev", axis=0, tiled=True)
+    sent = jnp.stack([aux_ft] * lax.axis_size("dev"))
+    gathered = jnp.concatenate(lax.all_to_all(sent, "dev", 0, 0), axis=0)
     blocks = item_pair
     images = item_image
     sub_ids = item_sub

time: 435 us -> 543 us (1.25)
  waiting for transfers between devices: 76.2 us -> 182 us
  between operations: 14.7 us -> 1.47 us
  starting transfers between devices: 0.01 us -> 11.9 us
  local copies, waits for them, and re-layouts: 56.5 us -> 65.4 us
    all_to_all x0 -> x1, waiting for transfers between devices: none -> 182 us  [body(): gathered = jnp.concatenate(lax.all_to_all(sent, 'dev', 0, 0), axis=0)]
    all_gather x1 -> x0, waiting for transfers between devices: 75.5 us -> none  [body(): gathered = lax.all_gather(aux_ft, 'dev', axis=0, tiled=True)]
    all_to_all x0 -> x1, starting transfers between devices: none -> 11.9 us  [body(): gathered = jnp.concatenate(lax.all_to_all(sent, 'dev', 0, 0), axis=0)]
    another operation x0 -> x1, local copies, waits for them, and re-layouts: none -> 9.52 us  [body(): sent = jnp.stack([aux_ft] * lax.axis_size('dev'))]
  transfers between devices with their start and end apart: 1 -> 1, of which waited for: 1 -> 1; matrix products, arithmetic and copies ran while one was open for 1% -> 0% of each run, Pallas kernels for 0% -> 0%
where the time goes in v1:
time: 543 us; the launch traced here: 542 us
  waiting for transfers between devices  182 us (34%)
  blocking collectives  171 us (31%)
  matrix products  95.2 us (18%)
  local copies, waits for them, and re-layouts  65.4 us (12%)
  starting transfers between devices  11.9 us (2%)
  other arithmetic  9.57 us (2%)
  loops' own time  5.67 us (1%)
    all_to_all x1, waiting for transfers between devices, body(): gathered = jnp.concatenate(lax.all_to_all(sent, 'dev', 0, 0), axis=0)  182 us
    unnamed x1, blocking collectives  171 us
    dot_general x8, matrix products, short_range(): jnp.einsum('pir,pci,is->pcsr', products, weights, placing, precision=lax....  64.2 us
    dot_general x8, matrix products, one_block(): jnp.dot(factor_rows, pair_matrix, preferred_element_type=jnp.float32)  15.8 us
    dynamic_slice x8, local copies, waits for them, and re-layouts, one_block(): lax.dynamic_slice_in_dim(factors, block_start - factor_offset, block_rows...  15.6 us
    dot_general x8, matrix products, short_range(): jnp.einsum('kp,ikr->pir', basis_cols, blocks, preferred_element_type=jnp....  14.8 us
    dynamic_update_slice x8, local copies, waits for them, and re-layouts, term_rows(): lax.map(one_block, jnp.arange(row_count // block_rows, dtype=jnp.int32))  14.5 us
    all_to_all x1, starting transfers between devices, body(): gathered = jnp.concatenate(lax.all_to_all(sent, 'dev', 0, 0), axis=0)  11.9 us
  transfers between devices with their start and end apart: 1, of which 1 were waited for; matrix products, arithmetic and copies ran while one was open for 0% of the time, Pallas kernels for 0%

profile of v1, /device:TPU:8, one launch (start us, length us, event | category | flops | bytes accessed | tf_op | source)
XLA Modules:
  0.0 542.0 jit_solution(17456101533653970043)
XLA Ops:
  0.0 9.5 %stack.10 = bf16[32,128,2,512]{3,2,1,0:T(2,128)(2,1)} broadcast(bf16[128,2,512]{2,1,0:T(2,128)(2,1)} %param.14), dimensions={1,2,3} | broadcast | bytes 8650752 | tf_op jit(solution)/shard_map/stack | solution.py:103
  9.6 11.9 %all-to-all-start = ((bf16[32,128,2,512]{3,2,1,0:T(2,128)(2,1)}), bf16[32,128,2,512]{3,2,1,0:T(2,128)(2,1)}, u32[]{:S(2)}, u32[]{:S(2)}) async-start(bf16[32,128,2,512]{3,2,1,0:T(2,128)(2,1)} %stack.10), calls=%async_computation | async-start | bytes 16777216 | tf_op jit(solution)/shard_map/all_to_all | solution.py:104
  24.2 1.2 maximum_maximum_fusion
  25.3 182.0 %all-to-all-done = bf16[32,128,2,512]{3,2,1,0:T(2,128)(2,1)} async-done(((bf16[32,128,2,512]{3,2,1,0:T(2,128)(2,1)}), bf16[32,128,2,512]{3,2,1,0:T(2,128)(2,1)}, u32[]{:S(2)}, u32[]{:S(2)}) %all-to-all-start) | async-done | bytes 8388640 | tf_op jit(solution)/shard_map/all_to_all | solution.py:104
  207.3 161.7 %while.14 = (s32[]{:T(128)}, f32[8,512,2,256]{3,2,1,0:T(2,128)}, s32[8]{0:T(128)S(1)}, bf16[4096,2,512]{2,1,0:T(2,128)(2,1)}, bf16[1024,512]{0,1:T(8,128)(2,1)},...) while((s32[]{:T(128)}, f32[8,512,2,256]{3,2,1,0:T(2,128)}, ...), condition=%wide.region_1.2_spmd, body=%wide.region_0.1_spmd.sunk | while | flops 855958080 | bytes 25042132 | solution.py:98
  208.6 0.8 dynamic-slice_negate_fusion.2
  209.7 1.8 convolution_bitcast_fusion.4
  211.6 8.0 %fusion.38 = f32[512,2,2,128]{3,1,2,0:T(2,128)S(1)} fusion(f32[512,16,128,1]{2,0,1,3:T(8,128)S(1)} %convolution_bitcast_fusion.4, f32[16,512,2]{0,2,1:T(2,128)S(1)} %multiply_bitcast_fusion.2, f32[16,2]{0,1:T(2,128)S(1)} %compare_convert_fusion.2), kind=kOutput, calls=%fused_computation.3.clone.1 | convolution fusion | flops 50364416 | bytes 5308544 | tf_op jit(solution)/shard_map/while/body/eval_jaxpr/pir,pci,is->pcsr/dot_general | solution.py:43
  220.2 0.8 reshape.92
  221.0 2.0 constant_dynamic-slice_fusion.2
  223.8 2.0 fusion.39
  225.7 1.9 copy_dynamic-update-slice_fusion.2
  228.8 0.8 dynamic-slice_negate_fusion.2
  230.0 1.8 convolution_bitcast_fusion.4
  231.9 8.0 %fusion.38 = f32[512,2,2,128]{3,1,2,0:T(2,128)S(1)} fusion(f32[512,16,128,1]{2,0,1,3:T(8,128)S(1)} %convolution_bitcast_fusion.4, f32[16,512,2]{0,2,1:T(2,128)S(1)} %multiply_bitcast_fusion.2, f32[16,2]{0,1:T(2,128)S(1)} %compare_convert_fusion.2), kind=kOutput, calls=%fused_computation.3.clone.1 | convolution fusion | flops 50364416 | bytes 5308544 | tf_op jit(solution)/shard_map/while/body/eval_jaxpr/pir,pci,is->pcsr/dot_general | solution.py:43
  240.5 0.8 reshape.92
  241.3 2.0 constant_dynamic-slice_fusion.2
  243.3 0.8 reshape.93
  244.0 2.0 fusion.39
  246.0 1.8 copy_dynamic-update-slice_fusion.2
  249.0 0.8 dynamic-slice_negate_fusion.2
  250.2 1.8 convolution_bitcast_fusion.4
  252.0 8.0 %fusion.38 = f32[512,2,2,128]{3,1,2,0:T(2,128)S(1)} fusion(f32[512,16,128,1]{2,0,1,3:T(8,128)S(1)} %convolution_bitcast_fusion.4, f32[16,512,2]{0,2,1:T(2,128)S(1)} %multiply_bitcast_fusion.2, f32[16,2]{0,1:T(2,128)S(1)} %compare_convert_fusion.2), kind=kOutput, calls=%fused_computation.3.clone.1 | convolution fusion | flops 50364416 | bytes 5308544 | tf_op jit(solution)/shard_map/while/body/eval_jaxpr/pir,pci,is->pcsr/dot_general | solution.py:43
  260.6 0.8 reshape.92
  261.5 2.0 constant_dynamic-slice_fusion.2
  264.2 2.0 fusion.39
  266.2 1.8 copy_dynamic-update-slice_fusion.2
  269.2 0.8 dynamic-slice_negate_fusion.2
  270.4 1.8 convolution_bitcast_fusion.4
  272.2 8.0 %fusion.38 = f32[512,2,2,128]{3,1,2,0:T(2,128)S(1)} fusion(f32[512,16,128,1]{2,0,1,3:T(8,128)S(1)} %convolution_bitcast_fusion.4, f32[16,512,2]{0,2,1:T(2,128)S(1)} %multiply_bitcast_fusion.2, f32[16,2]{0,1:T(2,128)S(1)} %compare_convert_fusion.2), kind=kOutput, calls=%fused_computation.3.clone.1 | convolution fusion | flops 50364416 | bytes 5308544 | tf_op jit(solution)/shard_map/while/body/eval_jaxpr/pir,pci,is->pcsr/dot_general | solution.py:43
  280.8 0.8 reshape.92
  281.7 2.0 constant_dynamic-slice_fusion.2
  284.4 2.0 fusion.39
  286.4 1.8 copy_dynamic-update-slice_fusion.2
  289.4 0.8 dynamic-slice_negate_fusion.2
  290.6 1.8 convolution_bitcast_fusion.4
  292.4 8.0 %fusion.38 = f32[512,2,2,128]{3,1,2,0:T(2,128)S(1)} fusion(f32[512,16,128,1]{2,0,1,3:T(8,128)S(1)} %convolution_bitcast_fusion.4, f32[16,512,2]{0,2,1:T(2,128)S(1)} %multiply_bitcast_fusion.2, f32[16,2]{0,1:T(2,128)S(1)} %compare_convert_fusion.2), kind=kOutput, calls=%fused_computation.3.clone.1 | convolution fusion | flops 50364416 | bytes 5308544 | tf_op jit(solution)/shard_map/while/body/eval_jaxpr/pir,pci,is->pcsr/dot_general | solution.py:43
  301.0 0.8 reshape.92
  301.9 2.0 constant_dynamic-slice_fusion.2
  304.6 2.0 fusion.39
  306.6 1.9 copy_dynamic-update-slice_fusion.2
  309.7 0.8 dynamic-slice_negate_fusion.2
  310.8 1.8 convolution_bitcast_fusion.4
  312.7 8.0 %fusion.38 = f32[512,2,2,128]{3,1,2,0:T(2,128)S(1)} fusion(f32[512,16,128,1]{2,0,1,3:T(8,128)S(1)} %convolution_bitcast_fusion.4, f32[16,512,2]{0,2,1:T(2,128)S(1)} %multiply_bitcast_fusion.2, f32[16,2]{0,1:T(2,128)S(1)} %compare_convert_fusion.2), kind=kOutput, calls=%fused_computation.3.clone.1 | convolution fusion | flops 50364416 | bytes 5308544 | tf_op jit(solution)/shard_map/while/body/eval_jaxpr/pir,pci,is->pcsr/dot_general | solution.py:43
  321.3 0.8 reshape.92
  322.1 2.0 constant_dynamic-slice_fusion.2
  324.9 2.0 fusion.39
  326.8 1.8 copy_dynamic-update-slice_fusion.2
  329.9 0.8 dynamic-slice_negate_fusion.2
  331.0 1.8 convolution_bitcast_fusion.4
  332.9 8.0 %fusion.38 = f32[512,2,2,128]{3,1,2,0:T(2,128)S(1)} fusion(f32[512,16,128,1]{2,0,1,3:T(8,128)S(1)} %convolution_bitcast_fusion.4, f32[16,512,2]{0,2,1:T(2,128)S(1)} %multiply_bitcast_fusion.2, f32[16,2]{0,1:T(2,128)S(1)} %compare_convert_fusion.2), kind=kOutput, calls=%fused_computation.3.clone.1 | convolution fusion | flops 50364416 | bytes 5308544 | tf_op jit(solution)/shard_map/while/body/eval_jaxpr/pir,pci,is->pcsr/dot_general | solution.py:43
  341.5 0.8 reshape.92
  342.3 2.0 constant_dynamic-slice_fusion.2
  345.0 2.0 fusion.39
  347.0 1.8 copy_dynamic-update-slice_fusion.2
  350.1 0.8 dynamic-slice_negate_fusion.2
  351.2 1.8 convolution_bitcast_fusion.4
  353.1 8.0 %fusion.38 = f32[512,2,2,128]{3,1,2,0:T(2,128)S(1)} fusion(f32[512,16,128,1]{2,0,1,3:T(8,128)S(1)} %convolution_bitcast_fusion.4, f32[16,512,2]{0,2,1:T(2,128)S(1)} %multiply_bitcast_fusion.2, f32[16,2]{0,1:T(2,128)S(1)} %compare_convert_fusion.2), kind=kOutput, calls=%fused_computation.3.clone.1 | convolution fusion | flops 50364416 | bytes 5308544 | tf_op jit(solution)/shard_map/while/body/eval_jaxpr/pir,pci,is->pcsr/dot_general | solution.py:43
  361.7 0.8 reshape.92
  362.5 2.0 constant_dynamic-slice_fusion.2
  365.2 2.0 fusion.39
  367.2 1.8 copy_dynamic-update-slice_fusion.2
  369.0 170.8 %all-reduce.2 = bf16[4096,2,256]{2,1,0:T(2,128)(2,1)} all-reduce(f32[4096,2,256]{2,1,0:T(2,128)} %bitcast.75), channel_id=2, replica_groups=mesh['grp'=8,'dev'=32] {'grp'}, use_global_device_ids=true, to_apply=%region_2.3.clone | all-reduce | flops 2097152 | bytes 12582912
  539.8 2.2 dynamic-slice_convert_fusion
  (78 shorter events, 18.8 us)
Async XLA Ops:
  0.0 23.5 %copy-start = (f32[125]{0:T(128)S(1)}, f32[125]{0:T(128)}, u32[]{:S(2)}) copy-start(f32[125]{0:T(128)} %param.19) | copy-start | bytes 1504
  9.5 12.6 %copy-start.6 = (u32[256]{0:T(256)S(1)}, u32[256]{0:T(256)}, u32[]{:S(2)}) copy-start(u32[256]{0:T(256)} %constant.47) | copy-start | bytes 3076
  9.5 14.0 %copy-start.3 = (s32[16]{0:T(128)S(1)}, s32[16]{0:T(128)}, u32[]{:S(2)}) copy-start(s32[16]{0:T(128)} %param.21) | copy-start | bytes 196
  9.5 14.3 %copy-start.4 = (f32[125]{0:T(128)S(1)}, f32[125]{0:T(128)}, u32[]{:S(2)}) copy-start(f32[125]{0:T(128)} %param.18) | copy-start | bytes 1504
  9.5 14.4 %copy-start.1 = (bf16[256,2,512]{2,1,0:T(2,128)(2,1)S(1)}, bf16[256,2,512]{2,1,0:T(2,128)(2,1)}, u32[]{:S(2)}) copy-start(bf16[256,2,512]{2,1,0:T(2,128)(2,1)} %param.13) | copy-start | bytes 1572868
  9.6 14.4 %copy-start.2 = (f32[512]{0:T(512)S(1)}, f32[512]{0:T(512)}, u32[]{:S(2)}) copy-start(f32[512]{0:T(512)} %param.15) | copy-start | bytes 6148
  9.6 197.8 %all-to-all-start = ((bf16[32,128,2,512]{3,2,1,0:T(2,128)(2,1)}), bf16[32,128,2,512]{3,2,1,0:T(2,128)(2,1)}, u32[]{:S(2)}, u32[]{:S(2)}) async-start(bf16[32,128,2,512]{3,2,1,0:T(2,128)(2,1)} %stack.10), calls=%async_computation | async-start | bytes 16777216 | tf_op jit(solution)/shard_map/all_to_all | solution.py:104
  21.5 185.9 %copy-start.5 = (s32[16]{0:T(128)S(1)}, s32[16]{0:T(128)}, u32[]{:S(2)}) copy-start(s32[16]{0:T(128)} %param.22) | copy-start | bytes 196
